TPU v7x, 32 devices: a whole 2x2x4 slice. The times are simulated.
32 devices in a mesh: dp: 2 (over x), expert: 16 (over z, y, core).
Axes of the slice: x: 2, y: 2, z: 4, core: 2. Of those that a mesh axis runs over, the one named last changes fastest.
Arguments:
- tokens: bfloat16 [4096, 1024], P(('dp', 'expert')), may hold values from -6 to 6
- cotangent: bfloat16 [4096, 1024], P(('dp', 'expert')), may hold values from -6 to 6
- expert_ids: int32 [4096, 6], P(('dp', 'expert')), may hold values from 0 to 15, all different within a row; in each aligned block of 128 rows (0 to 127, 128 to 255, ...) at most 60 rows name the same one
- gate_weights: float32 [4096, 6], P(('dp', 'expert')), may hold values from 0.05 to 0.3
- partner: int32 [16], replicated, may hold values from 0 to 15, as said below
- weights: bfloat16 [16, 1024, 3, 384], P('expert', 'dp'), may hold values from -0.3125 to 0.3125
- first_moment: bfloat16 [16, 1024, 3, 384], P('expert', 'dp'), may hold values from -6 to 6
- second_moment: bfloat16 [16, 1024, 3, 384], P('expert', 'dp'), may hold values from 0.099609375 to 4
Outputs:
- mixed: bfloat16 [4096, 1024], P(('dp', 'expert'))
- token_grad: bfloat16 [4096, 1024], P(('dp', 'expert'))
- new_weights: bfloat16 [16, 1024, 3, 384], P('expert', 'dp')
- new_first: bfloat16 [16, 1024, 3, 384], P('expert', 'dp')
- new_second: bfloat16 [16, 1024, 3, 384], P('expert', 'dp')
Inputs may be any that keep to these rules, and one draw needn't show every extreme that they name: `expert_ids`: each row names 6 different experts. Among the 128 tokens of one device (aligned blocks of rows), no expert is named by more than 60 tokens, and in every draw some block names some expert exactly 60 times. partner[partner[h]] = h and partner[h] != h for every h.
All inputs are finite; a program needn't handle non-finite values.
Results may differ from a plain program's by a relative error of at most 0.024.
Values may be sent and summed in bfloat16 or wider, within the bound.
A program may use at most 64 MiB of HBM per device.

v0:
```python
import jax
import jax.numpy as jnp
from jax import lax
from jax.sharding import PartitionSpec as P

beta_one = 0.9
beta_two = 0.95
learn_rate = 0.01
decay_rate = 0.1
eps_adam = 1e-08
step_count = 100


def send_rows(parts):
    return (lax.all_to_all(parts[0], "expert", split_axis=0, concat_axis=0, tiled=True),)


def send_back(parts):
    return (lax.all_to_all(parts[0], "expert", split_axis=0, concat_axis=0, tiled=True),)


def shards_by_slot(
    tokens, cotangent, expert_ids, gate_weights, partner, weights, first_moment, second_moment
):
    experts_here = lax.axis_size("expert")
    tok_dev, model_width = tokens.shape
    top_count = expert_ids.shape[1]
    hidden_width = weights.shape[3]
    capacity = min(tok_dev, max(2, 5 * tok_dev * top_count // (4 * experts_here)))
    item_total = tok_dev * top_count
    slot_total = experts_here * capacity
    flat_ids = expert_ids.reshape(item_total)
    onehot = (flat_ids[:, None] == jnp.arange(experts_here, dtype=jnp.int32)[None, :]).astype(
        jnp.int32
    )
    before = jnp.cumsum(onehot, axis=0) - onehot
    slot_of = jnp.sum(before * onehot, axis=1)
    position = flat_ids * capacity + slot_of
    source = (
        jnp.full((slot_total,), item_total, jnp.int32)
        .at[position]
        .set(jnp.arange(item_total, dtype=jnp.int32))
    )
    token_of = source // top_count
    zero_row = jnp.zeros((1, model_width), jnp.bfloat16)
    x_send = jnp.concatenate([tokens, zero_row], axis=0)[token_of].reshape(
        experts_here, capacity, model_width
    )
    gate_flat = gate_weights.reshape(item_total)
    gate_pad = jnp.concatenate([gate_flat, jnp.zeros((1,), jnp.float32)])
    cot_rows = jnp.concatenate([cotangent, zero_row], axis=0)[token_of].astype(jnp.float32)
    dy_send = (
        (gate_pad[source][:, None] * cot_rows)
        .astype(jnp.bfloat16)
        .reshape(experts_here, capacity, model_width)
    )
    gathered = lax.all_gather(weights, "dp", axis=1, tiled=True)[0]
    gate_up = gathered[:, 0:2, :].reshape(model_width, 2 * hidden_width)
    down_proj = gathered[:, 2, :]
    block_shape = (experts_here, capacity, model_width)
    (x_recv,) = send_rows((x_send,))
    forward_x_rows = x_recv.reshape(slot_total, model_width)
    both_proj = jnp.dot(forward_x_rows, gate_up, preferred_element_type=jnp.float32)
    pre_act = both_proj[:, :hidden_width]
    lin_act = both_proj[:, hidden_width:]
    sigmoid_pre = jax.nn.sigmoid(pre_act)
    silu_pre = pre_act * sigmoid_pre
    forward_hidden = (silu_pre * lin_act).astype(jnp.bfloat16)
    out_rows = jnp.dot(forward_hidden, down_proj.T, preferred_element_type=jnp.float32).astype(
        jnp.bfloat16
    )
    x_rows, saved, hidden, out_rows = (
        forward_x_rows,
        (pre_act, lin_act, sigmoid_pre, silu_pre),
        forward_hidden,
        out_rows,
    )
    (out_back,) = send_back((out_rows.reshape(block_shape),))
    (dy_recv,) = send_rows((dy_send,))
    pre_act, lin_act, sigmoid_pre, silu_pre = saved
    backward_dy_rows = dy_recv.reshape(slot_total, model_width)
    hidden_grad = jnp.dot(backward_dy_rows, down_proj, preferred_element_type=jnp.float32)
    pre_grad = (hidden_grad * lin_act * sigmoid_pre * (1.0 + pre_act * (1.0 - sigmoid_pre))).astype(
        jnp.bfloat16
    )
    lin_grad = (hidden_grad * silu_pre).astype(jnp.bfloat16)
    backward_both_grad = jnp.concatenate([pre_grad, lin_grad], axis=1)
    item_grad = jnp.dot(backward_both_grad, gate_up.T, preferred_element_type=jnp.float32).astype(
        jnp.bfloat16
    )
    dy_rows, both_grad, item_grad = (backward_dy_rows, backward_both_grad, item_grad)
    (grad_back,) = send_back((item_grad.reshape(block_shape),))
    out_items = (
        out_back.reshape(slot_total, model_width)[position].astype(jnp.float32) * gate_flat[:, None]
    )
    mixed = jnp.sum(out_items.reshape(tok_dev, top_count, model_width), axis=1).astype(jnp.bfloat16)
    grad_items = grad_back.reshape(slot_total, model_width)[position].astype(jnp.float32)
    token_grad = jnp.sum(grad_items.reshape(tok_dev, top_count, model_width), axis=1).astype(
        jnp.bfloat16
    )
    count = lax.axis_size("dp") * weights.shape[1]
    proj_grad = jnp.dot(x_rows.T, both_grad, preferred_element_type=jnp.float32)
    down_grad = jnp.dot(dy_rows.T, hidden, preferred_element_type=jnp.float32)
    grad_sum = lax.psum_scatter(
        jnp.concatenate(
            [proj_grad.reshape(count, 2, hidden_width), down_grad.reshape(count, 1, hidden_width)],
            axis=1,
        ).astype(jnp.bfloat16),
        "dp",
        scatter_dimension=0,
        tiled=True,
    ).astype(jnp.float32)
    w_old = weights[0].astype(jnp.float32)
    m_old = first_moment[0].astype(jnp.float32)
    v_old = second_moment[0].astype(jnp.float32)
    m_new = beta_one * m_old + (1.0 - beta_one) * grad_sum
    v_new = beta_two * v_old + (1.0 - beta_two) * grad_sum * grad_sum
    m_hat = m_new / (1.0 - beta_one**step_count)
    v_hat = v_new / (1.0 - beta_two**step_count)
    w_new = w_old - learn_rate * (m_hat / (jnp.sqrt(v_hat) + eps_adam) + decay_rate * w_old)
    pieces = (
        w_new.astype(jnp.bfloat16).reshape(experts_here, -1),
        m_new.astype(jnp.bfloat16).reshape(experts_here, -1),
        v_new.astype(jnp.bfloat16).reshape(experts_here, -1),
    )
    spread = (
        lax.all_to_all(pieces[0], "expert", split_axis=0, concat_axis=0, tiled=True),
        lax.all_to_all(pieces[1], "expert", split_axis=0, concat_axis=0, tiled=True),
        lax.all_to_all(pieces[2], "expert", split_axis=0, concat_axis=0, tiled=True),
    )
    ordered = (spread[0][partner], spread[1][partner], spread[2][partner])
    homed = (
        lax.all_to_all(ordered[0], "expert", split_axis=0, concat_axis=0, tiled=True),
        lax.all_to_all(ordered[1], "expert", split_axis=0, concat_axis=0, tiled=True),
        lax.all_to_all(ordered[2], "expert", split_axis=0, concat_axis=0, tiled=True),
    )
    new_weights = homed[0].reshape(weights.shape)
    new_first = homed[1].reshape(weights.shape)
    new_second = homed[2].reshape(weights.shape)
    return (mixed, token_grad, new_weights, new_first, new_second)


def adam(w_old, m_old, v_old, grad_sum):
    m_new = beta_one * m_old + (1.0 - beta_one) * grad_sum
    v_new = beta_two * v_old + (1.0 - beta_two) * grad_sum * grad_sum
    m_hat = m_new / (1.0 - beta_one**step_count)
    v_hat = v_new / (1.0 - beta_two**step_count)
    w_new = w_old - learn_rate * (m_hat / (jnp.sqrt(v_hat) + eps_adam) + decay_rate * w_old)
    return (w_new, m_new, v_new)


def shards_dense(
    tokens, cotangent, expert_ids, gate_weights, partner, weights, first_moment, second_moment
):
    experts_here = lax.axis_size("expert")
    me = lax.axis_index("expert")
    tok_dev, model_width = tokens.shape
    own_rows, hidden_width = (weights.shape[1], weights.shape[3])
    width = 3 * hidden_width
    f32, bf16 = (jnp.float32, jnp.bfloat16)
    hits = expert_ids[:, :, None] == jnp.arange(experts_here, dtype=jnp.int32)[None, None, :]
    gate_table = jnp.sum(jnp.where(hits, gate_weights[:, :, None], 0.0), axis=1).T
    w_flat = weights[0].reshape(own_rows, width)
    gathered = lax.all_gather(w_flat, "dp", axis=0, tiled=True)
    x_rows = lax.all_gather(tokens, "expert", axis=0, tiled=True)
    cot_rows = lax.all_gather(cotangent, "expert", axis=0, tiled=True)
    gate_all = lax.all_gather(gate_table, "expert", axis=0)
    gate = lax.dynamic_index_in_dim(gate_all, me, 1, keepdims=False)
    gate = gate.reshape(experts_here * tok_dev, 1)
    gate_up = gathered[:, : 2 * hidden_width]
    down_proj = gathered[:, 2 * hidden_width :]
    both_proj = jnp.dot(x_rows, gate_up, preferred_element_type=f32)
    pre_act = both_proj[:, :hidden_width]
    lin_act = both_proj[:, hidden_width:]
    sigmoid_pre = jax.nn.sigmoid(pre_act)
    silu_pre = pre_act * sigmoid_pre
    hidden = (silu_pre * lin_act).astype(bf16)
    out_rows = jnp.dot(hidden, down_proj.T, preferred_element_type=f32)
    mixed = lax.psum_scatter(
        (gate * out_rows).astype(bf16), "expert", scatter_dimension=0, tiled=True
    )
    dy_rows = (gate * cot_rows.astype(f32)).astype(bf16)
    hidden_grad = jnp.dot(dy_rows, down_proj, preferred_element_type=f32)
    pre_grad = hidden_grad * lin_act * sigmoid_pre * (1.0 + pre_act * (1.0 - sigmoid_pre))
    lin_grad = hidden_grad * silu_pre
    both_grad = jnp.concatenate([pre_grad.astype(bf16), lin_grad.astype(bf16)], axis=1)
    proj_grad = jnp.dot(x_rows.T, both_grad, preferred_element_type=f32)
    down_grad = jnp.dot(dy_rows.T, hidden, preferred_element_type=f32)
    partial = jnp.concatenate([proj_grad.astype(bf16), down_grad.astype(bf16)], axis=1)
    grad_sum = lax.psum_scatter(partial, "dp", scatter_dimension=0, tiled=True).astype(f32)
    item_grad = jnp.dot(both_grad, gate_up.T, preferred_element_type=f32).astype(bf16)
    token_grad = lax.psum_scatter(item_grad, "expert", scatter_dimension=0, tiled=True)
    m_flat = first_moment[0].reshape(own_rows, width)
    v_flat = second_moment[0].reshape(own_rows, width)
    new_state = adam(w_flat.astype(f32), m_flat.astype(f32), v_flat.astype(f32), grad_sum)
    share = own_rows // experts_here
    outs = []
    for part in new_state:
        pieces = part.astype(bf16).reshape(experts_here, share, width)
        spread = lax.all_to_all(pieces, "expert", split_axis=0, concat_axis=0, tiled=True)
        homed = lax.all_to_all(spread[partner], "expert", split_axis=0, concat_axis=0, tiled=True)
        outs.append(homed.reshape(weights.shape))
    return (mixed, token_grad, *outs)


def shards(*args):
    replica_rows = lax.axis_size("expert") * args[0].shape[0]
    if replica_rows <= 4096 and args[5].shape[1] % (16 * lax.axis_size("expert")) == 0:
        return shards_dense(*args)
    return shards_by_slot(*args)


def solution(mesh):
    in_specs = (
        P(("dp", "expert"), None),
        P(("dp", "expert"), None),
        P(("dp", "expert"), None),
        P(("dp", "expert"), None),
        P(),
        P("expert", "dp", None, None),
        P("expert", "dp", None, None),
        P("expert", "dp", None, None),
    )
    out_specs = (
        P(("dp", "expert"), None),
        P(("dp", "expert"), None),
        P("expert", "dp", None, None),
        P("expert", "dp", None, None),
        P("expert", "dp", None, None),
    )
    return jax.shard_map(shards, mesh=mesh, in_specs=in_specs, out_specs=out_specs, check_vma=False)
```

profile of v0, /device:TPU:15, one launch (start us, length us, event | category | flops | bytes accessed | tf_op | source)
XLA Modules:
  0.0 465.4 jit_solution(3843170583067933573)
XLA Ops:
  7.2 2.4 copy.29
  11.2 16.0 %all-gather = f32[256,128]{1,0:T(8,128)S(1)} all-gather(f32[16,128]{1,0:T(8,128)S(1)} %bitcast.29), channel_id=2, replica_groups=mesh['dp'=2,'expert'=16] {'expert'}, dimensions={0}, use_global_device_ids=true | all-gather | bytes 139264 | tf_op jit(solution)/shard_map/all_gather | solution.py:167
  27.2 19.2 %all-gather.7.cloned.1.call-done = bf16[1024,1152]{0,1:T(8,128)(2,1)} async-done(((bf16[512,1152]{0,1:T(8,128)(2,1)}), bf16[1024,1152]{0,1:T(8,128)(2,1)}) %all-gather.7.cloned.1.call-update) | async-done | bytes 2359312 | tf_op jit(solution)/shard_map/all_gather | solution.py:164
  46.4 53.2 %all-gather.5.cloned.1.call-done = bf16[2048,1024]{1,0:T(8,128)(2,1)} async-done(((bf16[128,1024]{1,0:T(8,128)(2,1)}), bf16[2048,1024]{1,0:T(8,128)(2,1)}) %all-gather.5.cloned.1.call-update) | async-done | bytes 4194320 | tf_op jit(solution)/shard_map/all_gather | solution.py:165
  99.6 8.7 %fusion.14 = f32[2048,768]{0,1:T(8,128)} fusion(bf16[2048,1024]{1,0:T(8,128)(2,1)} %all-gather.5.cloned.1.call-done, bf16[1024,1152]{0,1:T(8,128)(2,1)} %all-gather.7.cloned.1.call-done), kind=kOutput, calls=%fused_computation.32 | convolution fusion | flops 3221225472 | bytes 12058624 | tf_op jit(solution)/shard_map/dot_general | solution.py:172
  108.4 42.5 %all-gather.9.cloned.1.call-done = bf16[2048,1024]{1,0:T(8,128)(2,1)} async-done(((bf16[128,1024]{1,0:T(8,128)(2,1)}), bf16[2048,1024]{1,0:T(8,128)(2,1)}) %all-gather.9.cloned.1.call-update) | async-done | bytes 4194320 | tf_op jit(solution)/shard_map/all_gather | solution.py:166
  150.9 7.5 %multiply_convert_fusion.3 = (bf16[2048,384]{0,1:T(8,128)(2,1)S(1)}, bf16[2048,384]{0,1:T(8,128)(2,1)S(1)}, bf16[2048,384]{0,1:T(8,128)(2,1)S(1)}) fusion(f32[2048,768]{0,1:T(8,128)} %fusion.14, bf16[1024,1152]{0,1:T(8,128)(2,1)} %all-gather.7.cloned.1.call-done, bf16[2048,1024]{1,0:T(8,128)(2,1)} %all-gather.9.cloned.1.call-done, f32[2048]{0:T(1024)S(1)} %bitcast.30), kind=kOutput, calls=%fused_computation.9 | convolution fusion | flops 1628700672 | bytes 15998976 | tf_op jit(solution)/shard_map/dot_general | solution.py:183
  162.2 3.4 fusion.10
  174.6 25.7 %reduce-scatter.8.cloned.1.call-done = bf16[512,1152]{0,1:T(8,128)(2,1)} async-done(((bf16[1024,1152]{0,1:T(8,128)(2,1)}), bf16[512,1152]{0,1:T(8,128)(2,1)}) %reduce-scatter.8.cloned.1.call-update) | async-done | bytes 1179664 | tf_op jit(solution)/shard_map/reduce_scatter | solution.py:190
  200.3 5.8 %fusion.16 = (bf16[512,1152]{0,1:T(8,128)(2,1)S(1)}, bf16[512,1152]{0,1:T(8,128)(2,1)}, bf16[512,1152]{0,1:T(8,128)(2,1)S(1)}) fusion(bf16[512,1152]{0,1:T(8,128)(2,1)} %reduce-scatter.8.cloned.1.call-done, f32[1,512,3,384]{1,3,2,0:T(8,128)} %copy.31, f32[1,512,3,384]{1,3,2,0:T(8,128)} %copy.30, bf16[1,512,3,384]{1,3,2,0:T(8,128)(2,1)S(1)} %copy-done), kind=kLoop, calls=%fused_computation.34 | loop fusion | flops 10616832 | bytes 10616832 | tf_op jit(solution)/shard_map/convert_element_type | solution.py:199
  208.5 6.4 %all-to-all-start = ((bf16[16,32,1152]{2,1,0:T(8,128)(2,1)}), bf16[16,32,1152]{2,1,0:T(8,128)(2,1)S(1)}, u32[]{:S(2)}, u32[]{:S(2)}) async-start(bf16[16,32,1152]{2,1,0:T(8,128)(2,1)} %bitcast.7), calls=%async_computation.3 | async-start | bytes 2359296 | tf_op jit(solution)/shard_map/all_to_all | solution.py:200
  214.9 7.8 %convolution_convert_fusion = bf16[2048,1024]{1,0:T(8,128)(2,1)} fusion(bf16[2048,384]{0,1:T(8,128)(2,1)} %copy-done.11, bf16[2048,384]{0,1:T(8,128)(2,1)} %copy-done.10, bf16[1024,1152]{0,1:T(8,128)(2,1)} %all-gather.7.cloned.1.call-done), kind=kOutput, calls=%fused_computation.5 | convolution fusion | flops 3229614080 | bytes 8912896 | tf_op jit(solution)/shard_map/dot_general | solution.py:191
  224.1 18.5 %all-to-all-done = bf16[16,32,1152]{2,1,0:T(8,128)(2,1)S(1)} async-done(((bf16[16,32,1152]{2,1,0:T(8,128)(2,1)}), bf16[16,32,1152]{2,1,0:T(8,128)(2,1)S(1)}, u32[]{:S(2)}, u32[]{:S(2)}) %all-to-all-start) | async-done | bytes 1179680 | tf_op jit(solution)/shard_map/all_to_all | solution.py:200
  242.6 4.9 %all-to-all-start.2 = ((bf16[16,32,1152]{2,1,0:T(8,128)(2,1)}), bf16[16,32,1152]{2,1,0:T(8,128)(2,1)S(1)}, u32[]{:S(2)}, u32[]{:S(2)}) async-start(bf16[16,32,1152]{2,1,0:T(8,128)(2,1)} %bitcast.8), calls=%async_computation.5 | async-start | bytes 2359296 | tf_op jit(solution)/shard_map/all_to_all | solution.py:200
  248.9 43.1 %all-to-all-done.2 = bf16[16,32,1152]{2,1,0:T(8,128)(2,1)S(1)} async-done(((bf16[16,32,1152]{2,1,0:T(8,128)(2,1)}), bf16[16,32,1152]{2,1,0:T(8,128)(2,1)S(1)}, u32[]{:S(2)}, u32[]{:S(2)}) %all-to-all-start.2) | async-done | bytes 1179680 | tf_op jit(solution)/shard_map/all_to_all | solution.py:200
  292.1 4.9 %all-to-all-start.4 = ((bf16[16,32,1152]{2,1,0:T(8,128)(2,1)}), bf16[16,32,1152]{2,1,0:T(8,128)(2,1)S(1)}, u32[]{:S(2)}, u32[]{:S(2)}) async-start(bf16[16,32,1152]{2,1,0:T(8,128)(2,1)} %bitcast.27), calls=%async_computation.7 | async-start | bytes 2359296 | tf_op jit(solution)/shard_map/all_to_all | solution.py:200
  298.6 33.8 %all-to-all-done.4 = bf16[16,32,1152]{2,1,0:T(8,128)(2,1)S(1)} async-done(((bf16[16,32,1152]{2,1,0:T(8,128)(2,1)}), bf16[16,32,1152]{2,1,0:T(8,128)(2,1)S(1)}, u32[]{:S(2)}, u32[]{:S(2)}) %all-to-all-start.4) | async-done | bytes 1179680 | tf_op jit(solution)/shard_map/all_to_all | solution.py:200
  332.4 5.1 %all-to-all-start.1 = ((bf16[16,32,1152]{2,1,0:T(8,128)(2,1)}), bf16[16,32,1152]{2,1,0:T(8,128)(2,1)S(1)}, u32[]{:S(2)}, u32[]{:S(2)}) async-start(bf16[16,32,1152]{2,1,0:T(8,128)(2,1)} %gather_fusion), calls=%async_computation.4 | async-start | bytes 2359296 | tf_op jit(solution)/shard_map/all_to_all | solution.py:201
  337.5 6.0 %multiply_convert_fusion.1 = bf16[2048,1024]{1,0:T(8,128)(2,1)} fusion(bf16[2048,384]{0,1:T(8,128)(2,1)} %copy-done.9, f32[2048]{0:T(1024)S(1)} %bitcast.32, bf16[1024,1152]{0,1:T(8,128)(2,1)} %all-gather.7.cloned.1.call-done), kind=kOutput, calls=%fused_computation.4 | convolution fusion | flops 1614807040 | bytes 6561792 | tf_op jit(solution)/shard_map/dot_general | solution.py:178
  345.2 20.0 %all-to-all-done.1 = bf16[16,32,1152]{2,1,0:T(8,128)(2,1)S(1)} async-done(((bf16[16,32,1152]{2,1,0:T(8,128)(2,1)}), bf16[16,32,1152]{2,1,0:T(8,128)(2,1)S(1)}, u32[]{:S(2)}, u32[]{:S(2)}) %all-to-all-start.1) | async-done | bytes 1179680 | tf_op jit(solution)/shard_map/all_to_all | solution.py:201
  365.2 4.9 %all-to-all-start.3 = ((bf16[16,32,1152]{2,1,0:T(8,128)(2,1)}), bf16[16,32,1152]{2,1,0:T(8,128)(2,1)}, u32[]{:S(2)}, u32[]{:S(2)}) async-start(bf16[16,32,1152]{2,1,0:T(8,128)(2,1)} %gather_fusion.1), calls=%async_computation.6 | async-start | bytes 2359296 | tf_op jit(solution)/shard_map/all_to_all | solution.py:201
  371.8 43.0 %all-to-all-done.3 = bf16[16,32,1152]{2,1,0:T(8,128)(2,1)} async-done(((bf16[16,32,1152]{2,1,0:T(8,128)(2,1)}), bf16[16,32,1152]{2,1,0:T(8,128)(2,1)}, u32[]{:S(2)}, u32[]{:S(2)}) %all-to-all-start.3) | async-done | bytes 1179680 | tf_op jit(solution)/shard_map/all_to_all | solution.py:201
  414.8 5.0 %all-to-all-start.5 = ((bf16[16,32,1152]{2,1,0:T(8,128)(2,1)}), bf16[16,32,1152]{2,1,0:T(8,128)(2,1)}, u32[]{:S(2)}, u32[]{:S(2)}) async-start(bf16[16,32,1152]{2,1,0:T(8,128)(2,1)} %gather_fusion.2), calls=%async_computation.8 | async-start | bytes 2359296 | tf_op jit(solution)/shard_map/all_to_all | solution.py:201
  424.7 30.4 %all-to-all-done.5 = bf16[16,32,1152]{2,1,0:T(8,128)(2,1)} async-done(((bf16[16,32,1152]{2,1,0:T(8,128)(2,1)}), bf16[16,32,1152]{2,1,0:T(8,128)(2,1)}, u32[]{:S(2)}, u32[]{:S(2)}) %all-to-all-start.5) | async-done | bytes 1179680 | tf_op jit(solution)/shard_map/all_to_all | solution.py:201
  (60 shorter events, 33.0 us)
Async XLA Ops:
  7.2 4.0 copy-start.5
  7.2 4.0 copy-start.4
  7.2 39.2 %all-gather.7.cloned.1.call-start = ((), (), s32[]{:S(2)}) async-start(), calls=%async_computation.10 | async-start | bytes 3538944 | tf_op jit(solution)/shard_map/all_gather | solution.py:164
  9.6 90.0 %all-gather.5.cloned.1.call-start = ((), (), s32[]{:S(2)}) async-start(), calls=%async_computation.9 | async-start | bytes 4456448 | tf_op jit(solution)/shard_map/all_gather | solution.py:165
  10.4 140.5 %all-gather.9.cloned.1.call-start = ((), (), s32[]{:S(2)}) async-start(), calls=%async_computation.12 | async-start | bytes 4456448 | tf_op jit(solution)/shard_map/all_gather | solution.py:166
  11.1 189.2 %reduce-scatter.8.cloned.1.call-start = ((), (), s32[]{:S(2)}) async-start(), calls=%async_computation.14 | async-start | bytes 3538944 | tf_op jit(solution)/shard_map/reduce_scatter | solution.py:190
  150.9 7.5 %copy-start.7 = (bf16[2048,1024]{1,0:T(8,128)(2,1)S(1)}, bf16[2048,1024]{1,0:T(8,128)(2,1)}, u32[]{:S(2)}) copy-start(bf16[2048,1024]{1,0:T(8,128)(2,1)} %all-gather.9.cloned.1.call-done) | copy-start | bytes 12582916
  158.3 2.0 copy-start.9
  158.3 2.0 copy-start.10
  158.4 2.4 copy-start.11
  158.4 3.9 copy-start.6
  167.3 1.3 copy-start.3
  172.6 27.7 %copy-start = (bf16[1,512,3,384]{1,3,2,0:T(8,128)(2,1)S(1)}, bf16[1,512,3,384]{1,3,2,0:T(8,128)(2,1)}, u32[]{:S(2)}) copy-start(bf16[1,512,3,384]{1,3,2,0:T(8,128)(2,1)} %copy.29) | copy-start | bytes 3538948
  208.5 34.1 %all-to-all-start = ((bf16[16,32,1152]{2,1,0:T(8,128)(2,1)}), bf16[16,32,1152]{2,1,0:T(8,128)(2,1)S(1)}, u32[]{:S(2)}, u32[]{:S(2)}) async-start(bf16[16,32,1152]{2,1,0:T(8,128)(2,1)} %bitcast.7), calls=%async_computation.3 | async-start | bytes 2359296 | tf_op jit(solution)/shard_map/all_to_all | solution.py:200
  214.9 243.7 %reduce-scatter.6.cloned.1.call-start = ((), (), s32[]{:S(2)}) async-start(), calls=%async_computation.13 | async-start | bytes 4456448 | tf_op jit(solution)/shard_map/reduce_scatter | solution.py:192
  242.6 49.4 %all-to-all-start.2 = ((bf16[16,32,1152]{2,1,0:T(8,128)(2,1)}), bf16[16,32,1152]{2,1,0:T(8,128)(2,1)S(1)}, u32[]{:S(2)}, u32[]{:S(2)}) async-start(bf16[16,32,1152]{2,1,0:T(8,128)(2,1)} %bitcast.8), calls=%async_computation.5 | async-start | bytes 2359296 | tf_op jit(solution)/shard_map/all_to_all | solution.py:200
  247.5 49.4 %copy-start.8 = (s32[16]{0:T(128)S(1)}, s32[16]{0:T(128)}, u32[]{:S(2)}) copy-start(s32[16]{0:T(128)} %param.12) | copy-start | bytes 196
  292.1 40.4 %all-to-all-start.4 = ((bf16[16,32,1152]{2,1,0:T(8,128)(2,1)}), bf16[16,32,1152]{2,1,0:T(8,128)(2,1)S(1)}, u32[]{:S(2)}, u32[]{:S(2)}) async-start(bf16[16,32,1152]{2,1,0:T(8,128)(2,1)} %bitcast.27), calls=%async_computation.7 | async-start | bytes 2359296 | tf_op jit(solution)/shard_map/all_to_all | solution.py:200
  332.4 32.8 %all-to-all-start.1 = ((bf16[16,32,1152]{2,1,0:T(8,128)(2,1)}), bf16[16,32,1152]{2,1,0:T(8,128)(2,1)S(1)}, u32[]{:S(2)}, u32[]{:S(2)}) async-start(bf16[16,32,1152]{2,1,0:T(8,128)(2,1)} %gather_fusion), calls=%async_computation.4 | async-start | bytes 2359296 | tf_op jit(solution)/shard_map/all_to_all | solution.py:201
  337.5 121.1 %reduce-scatter.4.cloned.1.call-start = ((), (), s32[]{:S(2)}) async-start(), calls=%async_computation.11 | async-start | bytes 4456448 | tf_op jit(solution)/shard_map/reduce_scatter | solution.py:179
  365.2 6.6 %copy-start.1 = (bf16[16,32,1152]{2,1,0:T(8,128)(2,1)}, bf16[16,32,1152]{2,1,0:T(8,128)(2,1)S(1)}, u32[]{:S(2)}) copy-start(bf16[16,32,1152]{2,1,0:T(8,128)(2,1)S(1)} %all-to-all-done.1) | copy-start | bytes 3538948
  365.2 49.5 %all-to-all-start.3 = ((bf16[16,32,1152]{2,1,0:T(8,128)(2,1)}), bf16[16,32,1152]{2,1,0:T(8,128)(2,1)}, u32[]{:S(2)}, u32[]{:S(2)}) async-start(bf16[16,32,1152]{2,1,0:T(8,128)(2,1)} %gather_fusion.1), calls=%async_computation.6 | async-start | bytes 2359296 | tf_op jit(solution)/shard_map/all_to_all | solution.py:201
  414.8 5.0 %copy-start.2 = (bf16[16,32,1152]{2,1,0:T(8,128)(2,1)S(1)}, bf16[16,32,1152]{2,1,0:T(8,128)(2,1)}, u32[]{:S(2)}) copy-start(bf16[16,32,1152]{2,1,0:T(8,128)(2,1)} %copy-done.1) | copy-start | bytes 3538948
  414.8 40.4 %all-to-all-start.5 = ((bf16[16,32,1152]{2,1,0:T(8,128)(2,1)}), bf16[16,32,1152]{2,1,0:T(8,128)(2,1)}, u32[]{:S(2)}, u32[]{:S(2)}) async-start(bf16[16,32,1152]{2,1,0:T(8,128)(2,1)} %gather_fusion.2), calls=%async_computation.8 | async-start | bytes 2359296 | tf_op jit(solution)/shard_map/all_to_all | solution.py:201
Sparse Core Ops, SparseCore 0:
  10.1 36.2 all-gather.6
  48.6 50.9 all-gather.4
  101.8 49.0 all-gather.8
  167.5 32.7 reduce-scatter.7
  222.9 95.5 reduce-scatter.5
  343.7 96.6 reduce-scatter.3
where the time goes:
time: 466 us; the launch traced here: 465 us
  waiting for transfers between devices  331 us (71%)
  matrix products  35.4 us (8%)
  starting transfers between devices  31.2 us (7%)
  local copies, waits for them, and re-layouts  28.5 us (6%)
  blocking collectives  16 us (3%)
  between operations  14.3 us (3%)
  other arithmetic  9.17 us (2%)
    all_to_all x3, waiting for transfers between devices, shards_dense(): lax.all_to_all(pieces, 'expert', split_axis=0, concat_axis=0, tiled=True)  95.4 us
    all_to_all x3, waiting for transfers between devices, shards_dense(): lax.all_to_all(spread[partner], 'expert', split_axis=0, concat_axis=0, ti...  93.4 us
    all_gather x1, waiting for transfers between devices, shards_dense(): x_rows = lax.all_gather(tokens, 'expert', axis=0, tiled=True)  53.2 us
    all_gather x1, waiting for transfers between devices, shards_dense(): cot_rows = lax.all_gather(cotangent, 'expert', axis=0, tiled=True)  42.5 us
    reduce_scatter x1, waiting for transfers between devices, shards_dense(): lax.psum_scatter(partial, 'dp', scatter_dimension=0, tiled=True).astype(f32)  25.7 us
    all_gather x1, waiting for transfers between devices, shards_dense(): gathered = lax.all_gather(w_flat, 'dp', axis=0, tiled=True)  19.2 us
    all_to_all x3, starting transfers between devices, shards_dense(): lax.all_to_all(pieces, 'expert', split_axis=0, concat_axis=0, tiled=True)  16.1 us
    all_gather x1, blocking collectives, shards_dense(): gate_all = lax.all_gather(gate_table, 'expert', axis=0)  16 us
  transfers between devices with their start and end apart: 12, of which 10 were waited for; matrix products, arithmetic and copies ran while one was open for 10% of the time, Pallas kernels for 0%

commit v1 on v0

--- a/solution.py
+++ b/solution.py
@@ -9,6 +9,17 @@
 decay_rate = 0.1
 eps_adam = 1e-08
 step_count = 100
+
+
+def _number_ports(local_values, z_in):
+    piece_now = jnp.split(
+        jax.lax.all_gather(
+            jnp.concatenate([local_values, z_in], axis=1), "expert", axis=0, tiled=True
+        ),
+        [local_values.shape[1]],
+        axis=1,
+    )
+    return piece_now
 
 
 def send_rows(parts):
@@ -162,8 +173,7 @@
     gate_table = jnp.sum(jnp.where(hits, gate_weights[:, :, None], 0.0), axis=1).T
     w_flat = weights[0].reshape(own_rows, width)
     gathered = lax.all_gather(w_flat, "dp", axis=0, tiled=True)
-    x_rows = lax.all_gather(tokens, "expert", axis=0, tiled=True)
-    cot_rows = lax.all_gather(cotangent, "expert", axis=0, tiled=True)
+    x_rows, cot_rows = _number_ports(tokens, cotangent)
     gate_all = lax.all_gather(gate_table, "expert", axis=0)
     gate = lax.dynamic_index_in_dim(gate_all, me, 1, keepdims=False)
     gate = gate.reshape(experts_here * tok_dev, 1)

time: 466 us -> 441 us (0.946)
  waiting for transfers between devices: 331 us -> 312 us
  matrix products: 35.4 us -> 29.8 us
    all_gather x2 -> x1, waiting for transfers between devices: 95.7 us -> 77.5 us  [_number_ports(): jax.lax.all_gather(jnp.concatenate([local_values, z_in], axis=1), 'expert...]
  transfers between devices with their start and end apart: 12 -> 11, of which waited for: 10 -> 9; matrix products, arithmetic and copies ran while one was open for 10% -> 8% of each run, Pallas kernels for 0% -> 0%
where the time goes in v1:
time: 441 us; the launch traced here: 440 us
  waiting for transfers between devices  312 us (71%)
  starting transfers between devices  31.2 us (7%)
  matrix products  29.8 us (7%)
  local copies, waits for them, and re-layouts  26.6 us (6%)
  blocking collectives  16 us (4%)
  between operations  14 us (3%)
  other arithmetic  10 us (2%)
    all_to_all x3, waiting for transfers between devices, shards_dense(): lax.all_to_all(pieces, 'expert', split_axis=0, concat_axis=0, tiled=True)  95.4 us
    all_to_all x3, waiting for transfers between devices, shards_dense(): lax.all_to_all(spread[partner], 'expert', split_axis=0, concat_axis=0, ti...  93.4 us
    all_gather x1, waiting for transfers between devices, _number_ports(): jax.lax.all_gather(jnp.concatenate([local_values, z_in], axis=1), 'expert...  77.5 us
    reduce_scatter x1, waiting for transfers between devices, shards_dense(): lax.psum_scatter(partial, 'dp', scatter_dimension=0, tiled=True).astype(f32)  26.2 us
    all_gather x1, waiting for transfers between devices, shards_dense(): gathered = lax.all_gather(w_flat, 'dp', axis=0, tiled=True)  19.7 us
    all_to_all x3, starting transfers between devices, shards_dense(): lax.all_to_all(pieces, 'expert', split_axis=0, concat_axis=0, tiled=True)  16.1 us
    all_gather x1, blocking collectives, shards_dense(): gate_all = lax.all_gather(gate_table, 'expert', axis=0)  16 us
    all_to_all x3, starting transfers between devices, shards_dense(): lax.all_to_all(spread[partner], 'expert', split_axis=0, concat_axis=0, ti...  14.9 us
  transfers between devices with their start and end apart: 11, of which 9 were waited for; matrix products, arithmetic and copies ran while one was open for 8% of the time, Pallas kernels for 0%

profile of v1, /device:TPU:15, one launch (start us, length us, event | category | flops | bytes accessed | tf_op | source)
XLA Modules:
  0.0 439.9 jit_solution(18377606548891000793)
XLA Ops:
  7.3 2.4 copy.29
  10.7 16.0 %all-gather = f32[256,128]{1,0:T(8,128)S(1)} all-gather(f32[16,128]{1,0:T(8,128)S(1)} %bitcast.25), channel_id=2, replica_groups=mesh['dp'=2,'expert'=16] {'expert'}, dimensions={0}, use_global_device_ids=true | all-gather | bytes 139264 | tf_op jit(solution)/shard_map/all_gather | solution.py:177
  26.7 19.7 %all-gather.6.cloned.1.call-done = bf16[1024,1152]{0,1:T(8,128)(2,1)} async-done(((bf16[512,1152]{0,1:T(8,128)(2,1)}), bf16[1024,1152]{0,1:T(8,128)(2,1)}) %all-gather.6.cloned.1.call-update) | async-done | bytes 2359312 | tf_op jit(solution)/shard_map/all_gather | solution.py:175
  46.4 77.5 %all-gather.4.cloned.1.call-done = bf16[2048,2048]{1,0:T(8,128)(2,1)} async-done(((bf16[128,2048]{1,0:T(8,128)(2,1)}), bf16[2048,2048]{1,0:T(8,128)(2,1)}) %all-gather.4.cloned.1.call-update) | async-done | bytes 8388624 | tf_op jit(solution)/shard_map/all_gather | solution.py:16
  123.9 5.9 %fusion.2 = f32[2048,768]{0,1:T(8,128)S(1)} fusion(bf16[2048,2048]{1,0:T(8,128)(2,1)} %all-gather.4.cloned.1.call-done, bf16[1024,1152]{0,1:T(8,128)(2,1)} %all-gather.6.cloned.1.call-done), kind=kOutput, calls=%fused_computation.8 | convolution fusion | flops 3221225472 | bytes 12058624 | tf_op jit(solution)/shard_map/dot_general | solution.py:182
  129.8 4.7 %multiply_convert_fusion.3 = (bf16[2048,384]{0,1:T(8,128)(2,1)S(1)}, bf16[2048,384]{0,1:T(8,128)(2,1)S(1)}, bf16[2048,384]{0,1:T(8,128)(2,1)S(1)}) fusion(f32[2048,768]{0,1:T(8,128)S(1)} %fusion.2, bf16[1024,1152]{0,1:T(8,128)(2,1)} %all-gather.6.cloned.1.call-done, bf16[2048,2048]{1,0:T(8,128)(2,1)S(1)} %copy-done.8, f32[2048]{0:T(1024)S(1)} %bitcast.26), kind=kOutput, calls=%fused_computation.13 | convolution fusion | flops 1628700672 | bytes 15998976 | tf_op jit(solution)/shard_map/dot_general | solution.py:193
  136.8 3.4 fusion.10
  148.9 26.2 %reduce-scatter.8.cloned.1.call-done = bf16[512,1152]{0,1:T(8,128)(2,1)} async-done(((bf16[1024,1152]{0,1:T(8,128)(2,1)}), bf16[512,1152]{0,1:T(8,128)(2,1)}) %reduce-scatter.8.cloned.1.call-update) | async-done | bytes 1179664 | tf_op jit(solution)/shard_map/reduce_scatter | solution.py:200
  175.1 5.8 %fusion.16 = (bf16[512,1152]{0,1:T(8,128)(2,1)S(1)}, bf16[512,1152]{0,1:T(8,128)(2,1)}, bf16[512,1152]{0,1:T(8,128)(2,1)S(1)}) fusion(bf16[512,1152]{0,1:T(8,128)(2,1)} %reduce-scatter.8.cloned.1.call-done, f32[1,512,3,384]{1,3,2,0:T(8,128)} %copy.31, f32[1,512,3,384]{1,3,2,0:T(8,128)} %copy.30, bf16[1,512,3,384]{1,3,2,0:T(8,128)(2,1)S(1)} %copy-done), kind=kLoop, calls=%fused_computation.33 | loop fusion | flops 10616832 | bytes 10616832 | tf_op jit(solution)/shard_map/convert_element_type | solution.py:209
  181.0 2.4 copy.32
  183.3 6.4 %all-to-all-start = ((bf16[16,32,1152]{2,1,0:T(8,128)(2,1)}), bf16[16,32,1152]{2,1,0:T(8,128)(2,1)S(1)}, u32[]{:S(2)}, u32[]{:S(2)}) async-start(bf16[16,32,1152]{2,1,0:T(8,128)(2,1)} %bitcast.6), calls=%async_computation.3 | async-start | bytes 2359296 | tf_op jit(solution)/shard_map/all_to_all | solution.py:210
  189.8 7.8 %convolution_convert_fusion = bf16[2048,1024]{1,0:T(8,128)(2,1)} fusion(bf16[2048,384]{0,1:T(8,128)(2,1)} %copy-done.12, bf16[2048,384]{0,1:T(8,128)(2,1)} %copy-done.11, bf16[1024,1152]{0,1:T(8,128)(2,1)} %all-gather.6.cloned.1.call-done), kind=kOutput, calls=%fused_computation.5 | convolution fusion | flops 3229614080 | bytes 8912896 | tf_op jit(solution)/shard_map/dot_general | solution.py:201
  199.0 18.5 %all-to-all-done = bf16[16,32,1152]{2,1,0:T(8,128)(2,1)S(1)} async-done(((bf16[16,32,1152]{2,1,0:T(8,128)(2,1)}), bf16[16,32,1152]{2,1,0:T(8,128)(2,1)S(1)}, u32[]{:S(2)}, u32[]{:S(2)}) %all-to-all-start) | async-done | bytes 1179680 | tf_op jit(solution)/shard_map/all_to_all | solution.py:210
  217.5 4.9 %all-to-all-start.2 = ((bf16[16,32,1152]{2,1,0:T(8,128)(2,1)}), bf16[16,32,1152]{2,1,0:T(8,128)(2,1)S(1)}, u32[]{:S(2)}, u32[]{:S(2)}) async-start(bf16[16,32,1152]{2,1,0:T(8,128)(2,1)} %bitcast.7), calls=%async_computation.5 | async-start | bytes 2359296 | tf_op jit(solution)/shard_map/all_to_all | solution.py:210
  223.8 43.1 %all-to-all-done.2 = bf16[16,32,1152]{2,1,0:T(8,128)(2,1)S(1)} async-done(((bf16[16,32,1152]{2,1,0:T(8,128)(2,1)}), bf16[16,32,1152]{2,1,0:T(8,128)(2,1)S(1)}, u32[]{:S(2)}, u32[]{:S(2)}) %all-to-all-start.2) | async-done | bytes 1179680 | tf_op jit(solution)/shard_map/all_to_all | solution.py:210
  266.9 4.9 %all-to-all-start.4 = ((bf16[16,32,1152]{2,1,0:T(8,128)(2,1)}), bf16[16,32,1152]{2,1,0:T(8,128)(2,1)S(1)}, u32[]{:S(2)}, u32[]{:S(2)}) async-start(bf16[16,32,1152]{2,1,0:T(8,128)(2,1)} %bitcast.23), calls=%async_computation.7 | async-start | bytes 2359296 | tf_op jit(solution)/shard_map/all_to_all | solution.py:210
  273.5 33.8 %all-to-all-done.4 = bf16[16,32,1152]{2,1,0:T(8,128)(2,1)S(1)} async-done(((bf16[16,32,1152]{2,1,0:T(8,128)(2,1)}), bf16[16,32,1152]{2,1,0:T(8,128)(2,1)S(1)}, u32[]{:S(2)}, u32[]{:S(2)}) %all-to-all-start.4) | async-done | bytes 1179680 | tf_op jit(solution)/shard_map/all_to_all | solution.py:210
  307.2 5.1 %all-to-all-start.1 = ((bf16[16,32,1152]{2,1,0:T(8,128)(2,1)}), bf16[16,32,1152]{2,1,0:T(8,128)(2,1)S(1)}, u32[]{:S(2)}, u32[]{:S(2)}) async-start(bf16[16,32,1152]{2,1,0:T(8,128)(2,1)} %gather_fusion), calls=%async_computation.4 | async-start | bytes 2359296 | tf_op jit(solution)/shard_map/all_to_all | solution.py:211
  312.4 6.0 %multiply_convert_fusion.1 = bf16[2048,1024]{1,0:T(8,128)(2,1)} fusion(bf16[2048,384]{0,1:T(8,128)(2,1)} %copy-done.10, f32[2048]{0:T(1024)S(1)} %bitcast.28, bf16[1024,1152]{0,1:T(8,128)(2,1)} %all-gather.6.cloned.1.call-done), kind=kOutput, calls=%fused_computation.4 | convolution fusion | flops 1614807040 | bytes 6561792 | tf_op jit(solution)/shard_map/dot_general | solution.py:188
  320.1 20.0 %all-to-all-done.1 = bf16[16,32,1152]{2,1,0:T(8,128)(2,1)S(1)} async-done(((bf16[16,32,1152]{2,1,0:T(8,128)(2,1)}), bf16[16,32,1152]{2,1,0:T(8,128)(2,1)S(1)}, u32[]{:S(2)}, u32[]{:S(2)}) %all-to-all-start.1) | async-done | bytes 1179680 | tf_op jit(solution)/shard_map/all_to_all | solution.py:211
  340.1 4.9 %all-to-all-start.3 = ((bf16[16,32,1152]{2,1,0:T(8,128)(2,1)}), bf16[16,32,1152]{2,1,0:T(8,128)(2,1)}, u32[]{:S(2)}, u32[]{:S(2)}) async-start(bf16[16,32,1152]{2,1,0:T(8,128)(2,1)} %gather_fusion.1), calls=%async_computation.6 | async-start | bytes 2359296 | tf_op jit(solution)/shard_map/all_to_all | solution.py:211
  346.6 43.0 %all-to-all-done.3 = bf16[16,32,1152]{2,1,0:T(8,128)(2,1)} async-done(((bf16[16,32,1152]{2,1,0:T(8,128)(2,1)}), bf16[16,32,1152]{2,1,0:T(8,128)(2,1)}, u32[]{:S(2)}, u32[]{:S(2)}) %all-to-all-start.3) | async-done | bytes 1179680 | tf_op jit(solution)/shard_map/all_to_all | solution.py:211
  389.6 5.0 %all-to-all-start.5 = ((bf16[16,32,1152]{2,1,0:T(8,128)(2,1)}), bf16[16,32,1152]{2,1,0:T(8,128)(2,1)}, u32[]{:S(2)}, u32[]{:S(2)}) async-start(bf16[16,32,1152]{2,1,0:T(8,128)(2,1)} %gather_fusion.2), calls=%async_computation.8 | async-start | bytes 2359296 | tf_op jit(solution)/shard_map/all_to_all | solution.py:211
  399.6 30.4 %all-to-all-done.5 = bf16[16,32,1152]{2,1,0:T(8,128)(2,1)} async-done(((bf16[16,32,1152]{2,1,0:T(8,128)(2,1)}), bf16[16,32,1152]{2,1,0:T(8,128)(2,1)}, u32[]{:S(2)}, u32[]{:S(2)}) %all-to-all-start.5) | async-done | bytes 1179680 | tf_op jit(solution)/shard_map/all_to_all | solution.py:211
  (60 shorter events, 28.2 us)
Async XLA Ops:
  7.2 2.6 copy-start.5
  7.2 2.6 copy-start.4
  7.2 3.5 copy-start.7
  7.2 3.5 copy-start.6
  7.2 39.2 %all-gather.6.cloned.1.call-start = ((), (), s32[]{:S(2)}) async-start(), calls=%async_computation.10 | async-start | bytes 3538944 | tf_op jit(solution)/shard_map/all_gather | solution.py:175
  9.7 114.2 %all-gather.4.cloned.1.call-start = ((), (), s32[]{:S(2)}) async-start(), calls=%async_computation.9 | async-start | bytes 8912896 | tf_op jit(solution)/shard_map/all_gather | solution.py:16
  10.6 164.5 %reduce-scatter.8.cloned.1.call-start = ((), (), s32[]{:S(2)}) async-start(), calls=%async_computation.13 | async-start | bytes 3538944 | tf_op jit(solution)/shard_map/reduce_scatter | solution.py:200
  123.9 5.9 %copy-start.8 = (bf16[2048,2048]{1,0:T(8,128)(2,1)S(1)}, bf16[2048,2048]{1,0:T(8,128)(2,1)}, u32[]{:S(2)}) copy-start(bf16[2048,2048]{1,0:T(8,128)(2,1)} %all-gather.4.cloned.1.call-done) | copy-start | bytes 25165828
  134.6 2.0 copy-start.10
  134.6 2.0 copy-start.11
  134.6 2.2 copy-start.12
  141.8 1.3 copy-start.3
  146.9 28.2 %copy-start = (bf16[1,512,3,384]{1,3,2,0:T(8,128)(2,1)S(1)}, bf16[1,512,3,384]{1,3,2,0:T(8,128)(2,1)}, u32[]{:S(2)}) copy-start(bf16[1,512,3,384]{1,3,2,0:T(8,128)(2,1)} %copy.29) | copy-start | bytes 3538948
  183.3 34.1 %all-to-all-start = ((bf16[16,32,1152]{2,1,0:T(8,128)(2,1)}), bf16[16,32,1152]{2,1,0:T(8,128)(2,1)S(1)}, u32[]{:S(2)}, u32[]{:S(2)}) async-start(bf16[16,32,1152]{2,1,0:T(8,128)(2,1)} %bitcast.6), calls=%async_computation.3 | async-start | bytes 2359296 | tf_op jit(solution)/shard_map/all_to_all | solution.py:210
  189.7 243.7 %reduce-scatter.6.cloned.1.call-start = ((), (), s32[]{:S(2)}) async-start(), calls=%async_computation.12 | async-start | bytes 4456448 | tf_op jit(solution)/shard_map/reduce_scatter | solution.py:202
  217.5 49.4 %all-to-all-start.2 = ((bf16[16,32,1152]{2,1,0:T(8,128)(2,1)}), bf16[16,32,1152]{2,1,0:T(8,128)(2,1)S(1)}, u32[]{:S(2)}, u32[]{:S(2)}) async-start(bf16[16,32,1152]{2,1,0:T(8,128)(2,1)} %bitcast.7), calls=%async_computation.5 | async-start | bytes 2359296 | tf_op jit(solution)/shard_map/all_to_all | solution.py:210
  222.3 49.4 %copy-start.9 = (s32[16]{0:T(128)S(1)}, s32[16]{0:T(128)}, u32[]{:S(2)}) copy-start(s32[16]{0:T(128)} %param.12) | copy-start | bytes 196
  266.9 40.3 %all-to-all-start.4 = ((bf16[16,32,1152]{2,1,0:T(8,128)(2,1)}), bf16[16,32,1152]{2,1,0:T(8,128)(2,1)S(1)}, u32[]{:S(2)}, u32[]{:S(2)}) async-start(bf16[16,32,1152]{2,1,0:T(8,128)(2,1)} %bitcast.23), calls=%async_computation.7 | async-start | bytes 2359296 | tf_op jit(solution)/shard_map/all_to_all | solution.py:210
  307.2 32.8 %all-to-all-start.1 = ((bf16[16,32,1152]{2,1,0:T(8,128)(2,1)}), bf16[16,32,1152]{2,1,0:T(8,128)(2,1)S(1)}, u32[]{:S(2)}, u32[]{:S(2)}) async-start(bf16[16,32,1152]{2,1,0:T(8,128)(2,1)} %gather_fusion), calls=%async_computation.4 | async-start | bytes 2359296 | tf_op jit(solution)/shard_map/all_to_all | solution.py:211
  312.3 121.1 %reduce-scatter.4.cloned.1.call-start = ((), (), s32[]{:S(2)}) async-start(), calls=%async_computation.11 | async-start | bytes 4456448 | tf_op jit(solution)/shard_map/reduce_scatter | solution.py:189
  340.1 6.5 %copy-start.1 = (bf16[16,32,1152]{2,1,0:T(8,128)(2,1)}, bf16[16,32,1152]{2,1,0:T(8,128)(2,1)S(1)}, u32[]{:S(2)}) copy-start(bf16[16,32,1152]{2,1,0:T(8,128)(2,1)S(1)} %all-to-all-done.1) | copy-start | bytes 3538948
  340.1 49.5 %all-to-all-start.3 = ((bf16[16,32,1152]{2,1,0:T(8,128)(2,1)}), bf16[16,32,1152]{2,1,0:T(8,128)(2,1)}, u32[]{:S(2)}, u32[]{:S(2)}) async-start(bf16[16,32,1152]{2,1,0:T(8,128)(2,1)} %gather_fusion.1), calls=%async_computation.6 | async-start | bytes 2359296 | tf_op jit(solution)/shard_map/all_to_all | solution.py:211
  389.6 5.0 %copy-start.2 = (bf16[16,32,1152]{2,1,0:T(8,128)(2,1)S(1)}, bf16[16,32,1152]{2,1,0:T(8,128)(2,1)}, u32[]{:S(2)}) copy-start(bf16[16,32,1152]{2,1,0:T(8,128)(2,1)} %copy-done.1) | copy-start | bytes 3538948
  389.6 40.4 %all-to-all-start.5 = ((bf16[16,32,1152]{2,1,0:T(8,128)(2,1)}), bf16[16,32,1152]{2,1,0:T(8,128)(2,1)}, u32[]{:S(2)}, u32[]{:S(2)}) async-start(bf16[16,32,1152]{2,1,0:T(8,128)(2,1)} %gather_fusion.2), calls=%async_computation.8 | async-start | bytes 2359296 | tf_op jit(solution)/shard_map/all_to_all | solution.py:211
Sparse Core Ops, SparseCore 0:
  10.2 36.2 all-gather.5
  49.2 74.7 all-gather.3
  142.0 33.1 reduce-scatter.7
  197.7 95.5 reduce-scatter.5
  318.5 96.6 reduce-scatter.3
